TPU v7x, 32 devices: a whole 2x2x4 slice. The times are simulated.
32 devices in a mesh: row: 8 (over y, x, core), col: 4 (over z).
Axes of the slice: x: 2, y: 2, z: 4, core: 2. Of those that a mesh axis runs over, the one named last changes fastest.
Arguments:
- amplitudes: bfloat16 [4096, 4096], P('row', 'col'), may hold values from -0.1875 to 0.1875
- factors: bfloat16 [4096, 2048], P('col', 'row'), may hold values from -0.125 to 0.125
- tile_map: int32 [16, 16], P('row', 'col'), may hold values 0 or 1
- panel_owner: int32 [2], replicated, may hold values from 0 to 3, as said below
Outputs:
- cycle_term: float32 [4096, 4096], P('row', 'col')
Inputs may be any that keep to these rules, and one draw needn't show every extreme that they name: `panel_owner`: the 2 entries are distinct panel indices, and one of them is the last panel.
All inputs are finite; a program needn't handle non-finite values. No bound on the sum of `tile_map` on one device may be relied on, other than what follows from the above.
Results may differ from a plain program's by a relative error of at most 0.0029.
Values may be sent and summed in bfloat16 or wider, within the bound.
A program may use at most 64 MiB of HBM per device.

v0:
```python
import jax
import jax.numpy as jnp
from jax import lax
from jax.sharding import PartitionSpec as P


def spread(block, axis, owner):
    block = jnp.where(lax.axis_index(axis) == owner, block, jnp.zeros_like(block))
    return lax.psum(block, axis)


def keep_tiles(block, tiles):
    rows, cols = tiles.shape
    shaped = block.reshape(rows, block.shape[0] // rows, cols, block.shape[1] // cols)
    keep = tiles.astype(block.dtype)[:, None, :, None]
    return (shaped * keep).reshape(block.shape)


def outer_rows(left, right):
    return lax.dot_general(
        left, right, (((1,), (1,)), ((), ())), preferred_element_type=jnp.float32
    )


def shards(amplitudes, factors, tile_map, panel_owner):
    kept = keep_tiles(amplitudes, tile_map)
    width = factors.shape[0]
    total = jnp.zeros((kept.shape[0], width), jnp.float32)
    column_factors = lax.all_gather(factors, "row", axis=1, tiled=True)
    for step in range(panel_owner.shape[0]):
        owner = panel_owner[step]
        panel = spread(kept, "col", owner)
        owner_slice = spread(factors, "col", owner)
        owner_factors = lax.all_gather(owner_slice, "row", axis=1, tiled=True)
        integrals = outer_rows(owner_factors, column_factors).astype(jnp.bfloat16)
        total = total + jnp.dot(panel, integrals, preferred_element_type=jnp.float32)
    return keep_tiles(total, tile_map)


def solution(mesh):
    in_specs = (P("row", "col"), P("col", "row"), P("row", "col"), P())
    out_specs = P("row", "col")
    return jax.shard_map(shards, mesh=mesh, in_specs=in_specs, out_specs=out_specs, check_vma=False)
```

profile of v0, /device:TPU:0, one launch (start us, length us, event | category | flops | bytes accessed | tf_op | source)
XLA Modules:
  0.0 232.9 jit_solution(12405336362898462879)
XLA Ops:
  7.4 0.0 copy-start
  7.4 0.0 all-reduce.3.cloned.1.call-start
  7.4 0.8 fusion.10
  8.2 1.3 fusion.11
  9.4 0.3 mul.22
  9.8 0.2 copy.5
  11.2 2.1 broadcast_select_fusion.3
  13.3 0.0 copy-done
  13.3 1.5 broadcast_select_fusion.1
  14.8 0.0 all-reduce.3.cloned.1.call-update
  14.9 0.0 all-gather.6.cloned.1.call-start
  14.9 0.5 all-gather.6.cloned.1.call-update
  15.4 0.0 all-gather.8.cloned.1.call-start
  15.5 123.3 %all-reduce.3.cloned.1.call-done = (bf16[512,1024]{1,0:T(8,128)(2,1)}, bf16[1024,256]{1,0:T(8,128)(2,1)}, bf16[512,1024]{1,0:T(8,128)(2,1)}, bf16[1024,256]{1,0:T(8,128)(2,1)}) async-done(((bf16[512,1024]{1,0:T(8,128)(2,1)}, bf16[1024,256]{1,0:T(8,128)(2,1)}, bf16[512,1024]{1,0:T(8,128)(2,1)}, bf16[1024,256]{1,0:T(8,128)(2,1)}), (bf16[512,1024]{1,0:T(8,128)(2,1)}, bf16[1024,256]{1,0:T(8,128)(2,1)}, ...) | async-done | bytes 3145744 | tf_op jit(solution)/shard_map/psum | solution.py:9
  138.8 0.0 all-gather.8.cloned.1.call-update
  138.9 0.0 all-gather.4.cloned.1.call-start
  138.9 0.5 all-gather.4.cloned.1.call-update
  139.4 0.3 mul.25
  139.8 0.5 copy.6
  140.3 0.0 all-gather.6.cloned.1.call-done
  140.3 34.9 %all-gather.8.cloned.1.call-done = bf16[1024,2048]{1,0:T(8,128)(2,1)} async-done(((bf16[1024,256]{1,0:T(8,128)(2,1)}), bf16[1024,2048]{1,0:T(8,128)(2,1)}) %all-gather.8.cloned.1.call-update) | async-done | bytes 4194320 | tf_op jit(solution)/shard_map/all_gather | solution.py:34
  175.2 0.0 copy-start.1
  175.2 10.8 %fusion = f32[512,1024]{1,0:T(8,128)} fusion(bf16[512,1024]{1,0:T(8,128)(2,1)} %get-tuple-element.5, bf16[1024,2048]{1,0:T(8,128)(2,1)} %all-gather.8.cloned.1.call-done, bf16[1024,2048]{1,0:T(8,128)(2,1)} %all-gather.6.cloned.1.call-done), kind=kOutput, calls=%fused_computation.1 | convolution fusion | flops 5369757696 | bytes 11534336 | tf_op jit(solution)/shard_map/dot_general | solution.py:36
  186.0 28.2 %all-gather.4.cloned.1.call-done = bf16[1024,2048]{1,0:T(8,128)(2,1)} async-done(((bf16[1024,256]{1,0:T(8,128)(2,1)}), bf16[1024,2048]{1,0:T(8,128)(2,1)}) %all-gather.4.cloned.1.call-update) | async-done | bytes 4194320 | tf_op jit(solution)/shard_map/all_gather | solution.py:34
  214.2 0.0 copy-done.1
  214.2 11.1 %add_multiply_fusion = f32[512,1024]{1,0:T(8,128)} fusion(f32[512,1024]{1,0:T(8,128)S(1)} %bitcast.17, f32[512,1024]{1,0:T(8,128)} %fusion, bf16[512,1024]{1,0:T(8,128)(2,1)S(1)} %copy-done.1, bf16[1024,2048]{1,0:T(8,128)(2,1)} %all-gather.4.cloned.1.call-done, bf16[1024,2048]{1,0:T(8,128)(2,1)} %all-gather.6.cloned.1.call-done), kind=kOutput, calls=%fused_computation | convolution fusion | flops 5370806272 | bytes 15728640 | tf_op jit(solution)/shard_map/dot_general | solution.py:36
Async XLA Ops:
  7.4 6.0 %copy-start = (bf16[512,1024]{1,0:T(8,128)(2,1)S(1)}, bf16[512,1024]{1,0:T(8,128)(2,1)}, u32[]{:S(2)}) copy-start(bf16[512,1024]{1,0:T(8,128)(2,1)} %param.4) | copy-start | bytes 3145732
  7.4 131.5 %all-reduce.3.cloned.1.call-start = ((), (), s32[]{:S(2)}) async-start(), calls=%async_computation.3 | async-start | bytes 6291456 | tf_op jit(solution)/shard_map/psum | solution.py:9
  14.9 125.4 %all-gather.6.cloned.1.call-start = ((), (), s32[]{:S(2)}) async-start(), calls=%async_computation.1 | async-start | bytes 4718592 | tf_op jit(solution)/shard_map/all_gather | solution.py:29
  15.4 159.8 %all-gather.8.cloned.1.call-start = ((), (), s32[]{:S(2)}) async-start(), calls=%async_computation.2 | async-start | bytes 4718592 | tf_op jit(solution)/shard_map/all_gather | solution.py:34
  138.9 75.3 %all-gather.4.cloned.1.call-start = ((), (), s32[]{:S(2)}) async-start(), calls=%async_computation | async-start | bytes 4718592 | tf_op jit(solution)/shard_map/all_gather | solution.py:34
  175.2 39.0 %copy-start.1 = (bf16[512,1024]{1,0:T(8,128)(2,1)S(1)}, bf16[512,1024]{1,0:T(8,128)(2,1)}, u32[]{:S(2)}) copy-start(bf16[512,1024]{1,0:T(8,128)(2,1)} %get-tuple-element.7) | copy-start | bytes 3145732
Sparse Core Ops, SparseCore 0:
  15.0 123.8 all-reduce.2
Sparse Core Ops, SparseCore 1:
  17.2 39.9 all-gather.5
  139.0 36.2 all-gather.7
  177.0 37.2 all-gather.3
where the time goes:
time: 233 us
  waiting for transfers between devices  188 us (81%)
  matrix products  21.9 us (9%)
  between operations  16.3 us (7%)
  other arithmetic  4.41 us (2%)
  local copies, waits for them, and re-layouts  2.65 us (1%)
    psum x1, waiting for transfers between devices, spread(): return lax.psum(block, axis)  123 us
    all_gather x2, waiting for transfers between devices, shards(): owner_factors = lax.all_gather(owner_slice, 'row', axis=1, tiled=True)  63.1 us
    dot_general x2, matrix products, shards(): jnp.dot(panel, integrals, preferred_element_type=jnp.float32)  21.9 us
  transfers between devices with their start and end apart: 4, of which 3 were waited for; matrix products, arithmetic and copies ran while one was open for 5% of the time, Pallas kernels for 0%

commit v1 on v0

--- a/solution.py
+++ b/solution.py
@@ -4,9 +4,15 @@
 from jax.sharding import PartitionSpec as P
 
 
+def gather_and_add(block, axis):
+    terms = lax.all_gather(block, axis, axis=0, tiled=False)
+    result = terms.sum(axis=0)
+    return result
+
+
 def spread(block, axis, owner):
     block = jnp.where(lax.axis_index(axis) == owner, block, jnp.zeros_like(block))
-    return lax.psum(block, axis)
+    return gather_and_add(block, axis)
 
 
 def keep_tiles(block, tiles):

time: 233 us -> 402 us (1.73)
  waiting for transfers between devices: 188 us -> 344 us
  other arithmetic: 4.41 us -> 17.8 us
    all_gather x0 -> x4, waiting for transfers between devices: none -> 241 us  [gather_and_add(): terms = lax.all_gather(block, axis, axis=0, tiled=False)]
    psum x1 -> x0, waiting for transfers between devices: 123 us -> none  [spread(): return lax.psum(block, axis)]
    all_gather x1, waiting for transfers between devices: 0.03 us -> 34.3 us  [shards(): column_factors = lax.all_gather(factors, 'row', axis=1, tiled=True)]
    reduce_sum x0 -> x4, other arithmetic: none -> 13.4 us  [gather_and_add(): result = terms.sum(axis=0)]
    all_gather x2, waiting for transfers between devices: 63.1 us -> 67.6 us  [shards(): owner_factors = lax.all_gather(owner_slice, 'row', axis=1, tiled=True)]
  transfers between devices with their start and end apart: 4 -> 7, of which waited for: 3 -> 7; matrix products, arithmetic and copies ran while one was open for 5% -> 7% of each run, Pallas kernels for 0% -> 0%
where the time goes in v1:
time: 402 us
  waiting for transfers between devices  344 us (86%)
  matrix products  21.7 us (5%)
  other arithmetic  17.8 us (4%)
  between operations  14.8 us (4%)
    all_gather x4, waiting for transfers between devices, gather_and_add(): terms = lax.all_gather(block, axis, axis=0, tiled=False)  241 us
    all_gather x2, waiting for transfers between devices, shards(): owner_factors = lax.all_gather(owner_slice, 'row', axis=1, tiled=True)  67.6 us
    all_gather x1, waiting for transfers between devices, shards(): column_factors = lax.all_gather(factors, 'row', axis=1, tiled=True)  34.3 us
    dot_general x2, matrix products, shards(): jnp.dot(panel, integrals, preferred_element_type=jnp.float32)  21.7 us
    reduce_sum x4, other arithmetic, gather_and_add(): result = terms.sum(axis=0)  13.4 us
  transfers between devices with their start and end apart: 7, of which 7 were waited for; matrix products, arithmetic and copies ran while one was open for 7% of the time, Pallas kernels for 0%

profile of v1, /device:TPU:0, one launch (start us, length us, event | category | flops | bytes accessed | tf_op | source)
XLA Modules:
  0.0 401.6 jit_solution(3979388865257668337)
XLA Ops:
  6.5 1.4 fusion.11
  9.2 2.1 broadcast_select_fusion.3
  11.3 0.0 all-gather.24.cloned.1.call-update
  11.4 0.0 all-gather.20.cloned.1.call-start
  11.4 0.7 all-gather.20.cloned.1.call-update
  12.1 0.0 all-gather.22.cloned.1.call-start
  12.2 0.8 fusion.10
  12.9 0.3 mul.22
  13.3 0.2 copy.5
  13.5 1.5 broadcast_select_fusion.1
  15.0 0.0 all-gather.22.cloned.1.call-update
  15.0 0.0 all-gather.18.cloned.1.call-start
  15.1 0.5 all-gather.18.cloned.1.call-update
  15.6 0.0 all-gather.14.cloned.1.call-start
  15.6 0.5 all-gather.14.cloned.1.call-update
  16.2 0.0 all-gather.16.cloned.1.call-start
  16.2 43.7 %all-gather.24.cloned.1.call-done = bf16[4096,256]{1,0:T(8,128)(2,1)} async-done(((bf16[1024,256]{1,0:T(8,128)(2,1)}), bf16[4096,256]{1,0:T(8,128)(2,1)}) %all-gather.24.cloned.1.call-update) | async-done | bytes 2097168 | tf_op jit(solution)/shard_map/all_gather | solution.py:8
  59.9 2.8 reduce_sum.51
  62.8 0.0 all-gather.12.cloned.1.call-start
  62.8 43.1 %all-gather.20.cloned.1.call-done = bf16[4096,256]{1,0:T(8,128)(2,1)} async-done(((bf16[1024,256]{1,0:T(8,128)(2,1)}), bf16[4096,256]{1,0:T(8,128)(2,1)}) %all-gather.20.cloned.1.call-update) | async-done | bytes 2097168 | tf_op jit(solution)/shard_map/all_gather | solution.py:8
  106.0 2.9 reduce_sum.49
  108.9 0.3 mul.25
  109.2 0.5 copy.6
  109.7 77.4 %all-gather.22.cloned.1.call-done = bf16[2048,1024]{1,0:T(8,128)(2,1)} async-done(((bf16[512,1024]{1,0:T(8,128)(2,1)}), bf16[2048,1024]{1,0:T(8,128)(2,1)}) %all-gather.22.cloned.1.call-update) | async-done | bytes 4194320 | tf_op jit(solution)/shard_map/all_gather | solution.py:8
  187.1 4.4 %reduce_sum.50 = bf16[512,1024]{1,0:T(8,128)(2,1)} reduce(bf16[4,512,1024]{2,1,0:T(8,128)(2,1)} %bitcast.20, bf16[]{:T(256)} %constant.11.clone.1), dimensions={0}, to_apply=%region_2.3 | reduce | flops 1572864 | bytes 5242882 | tf_op jit(solution)/shard_map/reduce_sum | solution.py:9
  191.5 76.3 %all-gather.18.cloned.1.call-done = bf16[2048,1024]{1,0:T(8,128)(2,1)} async-done(((bf16[512,1024]{1,0:T(8,128)(2,1)}), bf16[2048,1024]{1,0:T(8,128)(2,1)}) %all-gather.18.cloned.1.call-update) | async-done | bytes 4194320 | tf_op jit(solution)/shard_map/all_gather | solution.py:8
  267.8 3.3 reduce_sum.48
  271.1 34.3 %all-gather.14.cloned.1.call-done = bf16[1024,2048]{1,0:T(8,128)(2,1)} async-done(((bf16[1024,256]{1,0:T(8,128)(2,1)}), bf16[1024,2048]{1,0:T(8,128)(2,1)}) %all-gather.14.cloned.1.call-update) | async-done | bytes 4194320 | tf_op jit(solution)/shard_map/all_gather | solution.py:35
  305.4 39.1 %all-gather.16.cloned.1.call-done = bf16[1024,2048]{1,0:T(8,128)(2,1)} async-done(((bf16[1024,256]{1,0:T(8,128)(2,1)}), bf16[1024,2048]{1,0:T(8,128)(2,1)}) %all-gather.16.cloned.1.call-update) | async-done | bytes 4194320 | tf_op jit(solution)/shard_map/all_gather | solution.py:40
  344.5 10.7 %fusion = f32[512,1024]{1,0:T(8,128)} fusion(bf16[512,1024]{1,0:T(8,128)(2,1)} %reduce_sum.50, bf16[1024,2048]{1,0:T(8,128)(2,1)} %all-gather.16.cloned.1.call-done, bf16[1024,2048]{1,0:T(8,128)(2,1)} %all-gather.14.cloned.1.call-done), kind=kOutput, calls=%fused_computation.1 | convolution fusion | flops 5369757696 | bytes 11534336 | tf_op jit(solution)/shard_map/dot_general | solution.py:42
  355.2 28.5 %all-gather.12.cloned.1.call-done = bf16[1024,2048]{1,0:T(8,128)(2,1)} async-done(((bf16[1024,256]{1,0:T(8,128)(2,1)}), bf16[1024,2048]{1,0:T(8,128)(2,1)}) %all-gather.12.cloned.1.call-update) | async-done | bytes 4194320 | tf_op jit(solution)/shard_map/all_gather | solution.py:40
  383.7 11.0 %add_multiply_fusion = f32[512,1024]{1,0:T(8,128)} fusion(f32[512,1024]{1,0:T(8,128)S(1)} %bitcast.25, f32[512,1024]{1,0:T(8,128)} %fusion, bf16[512,1024]{1,0:T(8,128)(2,1)S(1)} %reduce_sum.48, bf16[1024,2048]{1,0:T(8,128)(2,1)} %all-gather.12.cloned.1.call-done, bf16[1024,2048]{1,0:T(8,128)(2,1)} %all-gather.14.cloned.1.call-done), kind=kOutput, calls=%fused_computation | convolution fusion | flops 5370806272 | bytes 15728640 | tf_op jit(solution)/shard_map/dot_general | solution.py:42
  (5 shorter events, 0.0 us)
Async XLA Ops:
  6.5 7.0 %copy-start = (bf16[512,1024]{1,0:T(8,128)(2,1)S(1)}, bf16[512,1024]{1,0:T(8,128)(2,1)}, u32[]{:S(2)}) copy-start(bf16[512,1024]{1,0:T(8,128)(2,1)} %param.4) | copy-start | bytes 3145732
  6.5 53.4 %all-gather.24.cloned.1.call-start = ((), (), s32[]{:S(2)}) async-start(), calls=%async_computation.6 | async-start | bytes 2621440 | tf_op jit(solution)/shard_map/all_gather | solution.py:8
  11.4 94.6 %all-gather.20.cloned.1.call-start = ((), (), s32[]{:S(2)}) async-start(), calls=%async_computation.4 | async-start | bytes 2621440 | tf_op jit(solution)/shard_map/all_gather | solution.py:8
  12.1 175.0 %all-gather.22.cloned.1.call-start = ((), (), s32[]{:S(2)}) async-start(), calls=%async_computation.5 | async-start | bytes 5242880 | tf_op jit(solution)/shard_map/all_gather | solution.py:8
  15.0 252.8 %all-gather.18.cloned.1.call-start = ((), (), s32[]{:S(2)}) async-start(), calls=%async_computation.3 | async-start | bytes 5242880 | tf_op jit(solution)/shard_map/all_gather | solution.py:8
  15.6 289.8 %all-gather.14.cloned.1.call-start = ((), (), s32[]{:S(2)}) async-start(), calls=%async_computation.1 | async-start | bytes 4718592 | tf_op jit(solution)/shard_map/all_gather | solution.py:35
  16.2 328.3 %all-gather.16.cloned.1.call-start = ((), (), s32[]{:S(2)}) async-start(), calls=%async_computation.2 | async-start | bytes 4718592 | tf_op jit(solution)/shard_map/all_gather | solution.py:40
  62.8 321.0 %all-gather.12.cloned.1.call-start = ((), (), s32[]{:S(2)}) async-start(), calls=%async_computation | async-start | bytes 4718592 | tf_op jit(solution)/shard_map/all_gather | solution.py:40
Sparse Core Ops, SparseCore 0:
  11.5 48.3 all-gather.23
  61.5 44.4 all-gather.19
  107.5 79.5 all-gather.21
  188.5 79.2 all-gather.17
  269.5 35.8 all-gather.13
  307.1 37.3 all-gather.15
  346.4 37.3 all-gather.11
